TPU v7x, 256 devices: a whole 4x4x8 slice. The times are simulated.
256 devices in a mesh: out: 128 (over z, y, x), con: 2 (over core).
Axes of the slice: x: 4, y: 4, z: 8, core: 2. Of those that a mesh axis runs over, the one named last changes fastest.
Arguments:
- amplitudes: bfloat16 [512, 9216], P(('out', 'con')), may hold values from -6 to 6
- integrals: bfloat16 [131072, 9216], P('out', 'con'), may hold values from -0.078125 to 0.078125
- block_sizes: int32 [8], replicated, may hold values from 64 to 192, as said below
Outputs:
- ladder: bfloat16 [512, 131072], P('con', 'out')
Inputs may be any that keep to these rules, and one draw needn't show every extreme that they name: `block_sizes`: each entry lies between 64 and 192; the entries sum to 1024; one entry equals 192 and one equals 64.
All inputs are finite; a program needn't handle non-finite values.
Results may differ from a plain program's by a relative error of at most 0.001.
Values may be sent and summed in bfloat16 or wider, within the bound.
A program may use at most 64 MiB of HBM per device.

v0:
```python
import jax
import jax.numpy as jnp
from jax import lax
from jax.sharding import PartitionSpec as P

DMAX = 192


def mask_slots(amplitudes, block_sizes):
    row_count = amplitudes.shape[0]
    nirrep = block_sizes.shape[0]
    blocked = amplitudes.reshape(row_count, nirrep, -1, DMAX)
    valid_cols = jnp.arange(DMAX, dtype=jnp.int32)[None, :] < block_sizes[:, None]
    masked = jnp.where(valid_cols[None, :, None, :], blocked, jnp.zeros((), amplitudes.dtype))
    return masked.reshape(row_count, -1)


def contract(amp_rows, integrals):
    return lax.dot_general(
        amp_rows, integrals, (((1,), (1,)), ((), ())), preferred_element_type=jnp.float32
    )


def on_device(amplitudes, integrals, block_sizes):
    masked = mask_slots(amplitudes, block_sizes)
    con = lax.axis_index("con")
    con_count = lax.axis_size("con")
    half = integrals.shape[1]
    chip_rows = lax.all_gather(masked, "con", axis=0, tiled=True)
    own_cols = lax.dynamic_slice_in_dim(chip_rows, con * half, half, axis=1)
    all_rows = lax.all_gather(own_cols, "out", axis=0, tiled=True)
    out_rows = all_rows.shape[0] // con_count
    other = 1 - con
    other_part = contract(
        lax.dynamic_slice_in_dim(all_rows, other * out_rows, out_rows, axis=0), integrals
    )
    received = lax.ppermute(other_part, "con", perm=[(0, 1), (1, 0)])
    own_part = contract(
        lax.dynamic_slice_in_dim(all_rows, con * out_rows, out_rows, axis=0), integrals
    )
    own_part = lax.optimization_barrier(own_part)
    return (own_part + received).astype(jnp.bfloat16)


def solution(mesh):
    in_specs = (P(("out", "con"), None), P("out", "con"), P())
    out_specs = P("con", "out")
    return jax.shard_map(
        on_device, mesh=mesh, in_specs=in_specs, out_specs=out_specs, check_vma=False
    )
```

profile of v0, /device:TPU:1, one launch (start us, length us, event | category | flops | bytes accessed | tf_op | source)
XLA Modules:
  0.0 160.5 jit_solution(4676826917405376229)
XLA Ops:
  6.5 0.0 all-gather.4.cloned.1.call-start
  6.5 0.7 iota_compare_fusion
  7.3 0.1 broadcast_in_dim.20
  7.4 0.8 fusion.4
  8.2 4.8 %all-gather = bf16[2,2,9216]{2,1,0:T(2,128)(2,1)S(1)} all-gather(bf16[1,2,9216]{2,1,0:T(2,128)(2,1)S(1)} %fusion.4), channel_id=1, replica_groups=mesh['out'=128,'con'=2] {'con'}, dimensions={0}, use_global_device_ids=true | all-gather | bytes 110592 | tf_op jit(solution)/shard_map/all_gather | solution.py:29
  13.0 0.6 dynamic-slice_bitcast_fusion
  13.7 0.0 all-gather.4.cloned.1.call-update
  13.7 115.3 %all-gather.4.cloned.1.call-done = bf16[128,4,4608]{2,1,0:T(4,128)(2,1)} async-done(((bf16[1,4,4608]{2,1,0:T(4,128)(2,1)}), bf16[128,4,4608]{2,1,0:T(4,128)(2,1)}) %all-gather.4.cloned.1.call-update) | async-done | bytes 4718608 | tf_op jit(solution)/shard_map/all_gather | solution.py:31
  129.0 7.2 %reshape.24 = bf16[512,4608]{1,0:T(8,128)(2,1)} reshape(bf16[128,4,4608]{2,1,0:T(4,128)(2,1)} %all-gather.4.cloned.1.call-done) | data formatting | bytes 9437184
  136.2 6.0 %fusion = f32[256,1024]{1,0:T(8,128)S(1)} fusion(bf16[1024,4608]{1,0:T(8,128)(2,1)} %param.4, bf16[512,4608]{1,0:T(8,128)(2,1)} %reshape.24, s32[]{:T(128)S(6)} %select_n.17), kind=kOutput, calls=%fused_computation | convolution fusion | flops 2415919104 | bytes 12845060 | tf_op jit(solution)/shard_map/dot_general | solution.py:19
  142.2 4.5 %collective-permute-start = (f32[256,1024]{1,0:T(8,128)S(1)}, f32[256,1024]{1,0:T(8,128)S(1)}, u32[]{:S(2)}, u32[]{:S(2)}) collective-permute-start(f32[256,1024]{1,0:T(8,128)S(1)} %fusion), channel_id=1, source_target_pairs={{0,1},{1,0},{2,3},{3,2},{4,5},{5,4},{6,7},{7,6},{8,9},{9,8},{10,11... | collective-permute-start | bytes 3145736 | tf_op jit(solution)/shard_map/ppermute | solution.py:37
  146.7 6.0 %fusion.2 = f32[256,1024]{1,0:T(8,128)S(1)} fusion(bf16[1024,4608]{1,0:T(8,128)(2,1)} %param.4, bf16[512,4608]{1,0:T(8,128)(2,1)} %reshape.24, s32[]{:T(128)S(6)} %select_n.16), kind=kOutput, calls=%fused_computation.2 | convolution fusion | flops 2415919104 | bytes 12845060 | tf_op jit(solution)/shard_map/dot_general | solution.py:19
  152.7 0.0 collective-permute-done
  152.7 1.0 add_convert_fusion
  (2 shorter events, 0.0 us)
Async XLA Ops:
  6.5 122.5 %all-gather.4.cloned.1.call-start = ((), (), s32[]{:S(2)}) async-start(), calls=%async_computation | async-start | bytes 4755456 | tf_op jit(solution)/shard_map/all_gather | solution.py:31
  142.2 10.5 %collective-permute-start = (f32[256,1024]{1,0:T(8,128)S(1)}, f32[256,1024]{1,0:T(8,128)S(1)}, u32[]{:S(2)}, u32[]{:S(2)}) collective-permute-start(f32[256,1024]{1,0:T(8,128)S(1)} %fusion), channel_id=1, source_target_pairs={{0,1},{1,0},{2,3},{3,2},{4,5},{5,4},{6,7},{7,6},{8,9},{9,8},{10,11... | collective-permute-start | bytes 3145736 | tf_op jit(solution)/shard_map/ppermute | solution.py:37
Sparse Core Ops, SparseCore 0:
  13.8 115.1 all-gather.3
where the time goes:
time: 161 us; the launch traced here: 160 us
  waiting for transfers between devices  115 us (71%)
  between operations  13.4 us (8%)
  matrix products  11.9 us (7%)
  local copies, waits for them, and re-layouts  8.04 us (5%)
  blocking collectives  4.75 us (3%)
  starting transfers between devices  4.49 us (3%)
  other arithmetic  2.51 us (2%)
    all_gather x1, waiting for transfers between devices, on_device(): all_rows = lax.all_gather(own_cols, 'out', axis=0, tiled=True)  115 us
    dot_general x2, matrix products, contract(): lax.dot_general(amp_rows, integrals, (((1,), (1,)), ((), ())), preferred_...  11.9 us
    unnamed x3, local copies, waits for them, and re-layouts  7.92 us
    all_gather x1, blocking collectives, on_device(): chip_rows = lax.all_gather(masked, 'con', axis=0, tiled=True)  4.75 us
    ppermute x1, starting transfers between devices, on_device(): received = lax.ppermute(other_part, 'con', perm=[(0, 1), (1, 0)])  4.49 us
  transfers between devices with their start and end apart: 2, of which 1 were waited for; matrix products, arithmetic and copies ran while one was open for 4% of the time, Pallas kernels for 0%

commit v1 on v0

--- a/solution.py
+++ b/solution.py
@@ -26,7 +26,9 @@
     con = lax.axis_index("con")
     con_count = lax.axis_size("con")
     half = integrals.shape[1]
-    chip_rows = lax.all_gather(masked, "con", axis=0, tiled=True)
+    chip_rows = jnp.concatenate(
+        jax.lax.all_to_all(jnp.stack([masked] * jax.lax.axis_size("con")), "con", 0, 0), 0
+    )
     own_cols = lax.dynamic_slice_in_dim(chip_rows, con * half, half, axis=1)
     all_rows = lax.all_gather(own_cols, "out", axis=0, tiled=True)
     out_rows = all_rows.shape[0] // con_count

time: 161 us -> 167 us (1.037)
  starting transfers between devices: 4.49 us -> 11 us
  blocking collectives: 4.75 us -> 0 us
  waiting for transfers between devices: 115 us -> 119 us
    all_to_all x0 -> x1, starting transfers between devices: none -> 6.54 us  [on_device(): jax.lax.all_to_all(jnp.stack([masked] * jax.lax.axis_size('con')), 'con',...]
    all_gather x1 -> x0, blocking collectives: 4.75 us -> none  [on_device(): chip_rows = lax.all_gather(masked, 'con', axis=0, tiled=True)]
    all_gather x1, waiting for transfers between devices: 115 us -> 118 us  [on_device(): all_rows = lax.all_gather(own_cols, 'out', axis=0, tiled=True)]
    unnamed x3 -> x2, local copies, waits for them, and re-layouts: 7.92 us -> 7.87 us
  transfers between devices with their start and end apart: 2 -> 3, of which waited for: 1 -> 2; matrix products, arithmetic and copies ran while one was open for 4% -> 4% of each run, Pallas kernels for 0% -> 0%
where the time goes in v1:
time: 167 us; the launch traced here: 166 us
  waiting for transfers between devices  119 us (71%)
  between operations  13.4 us (8%)
  matrix products  11.9 us (7%)
  starting transfers between devices  11 us (7%)
  local copies, waits for them, and re-layouts  8.03 us (5%)
  other arithmetic  3.2 us (2%)
    all_gather x1, waiting for transfers between devices, on_device(): all_rows = lax.all_gather(own_cols, 'out', axis=0, tiled=True)  118 us
    dot_general x2, matrix products, contract(): lax.dot_general(amp_rows, integrals, (((1,), (1,)), ((), ())), preferred_...  11.9 us
    unnamed x2, local copies, waits for them, and re-layouts  7.87 us
    all_to_all x1, starting transfers between devices, on_device(): jax.lax.all_to_all(jnp.stack([masked] * jax.lax.axis_size('con')), 'con',...  6.54 us
    ppermute x1, starting transfers between devices, on_device(): received = lax.ppermute(other_part, 'con', perm=[(0, 1), (1, 0)])  4.5 us
  transfers between devices with their start and end apart: 3, of which 2 were waited for; matrix products, arithmetic and copies ran while one was open for 4% of the time, Pallas kernels for 0%

profile of v1, /device:TPU:1, one launch (start us, length us, event | category | flops | bytes accessed | tf_op | source)
XLA Modules:
  0.0 166.3 jit_solution(18214157720322139895)
XLA Ops:
  6.5 0.7 iota_compare_fusion
  7.3 0.1 broadcast_in_dim.20
  7.4 0.8 fusion.4
  8.2 0.7 pad_maximum_fusion
  8.9 6.5 %all-to-all-start = ((bf16[2,2,9216]{2,1,0:T(2,128)(2,1)}), bf16[2,2,9216]{2,1,0:T(2,128)(2,1)S(1)}, u32[]{:S(2)}, u32[]{:S(2)}) async-start(bf16[2,2,9216]{2,1,0:T(2,128)(2,1)} %pad_maximum_fusion), calls=%async_computation | async-start | bytes 147456 | tf_op jit(solution)/shard_map/all_to_all | solution.py:30
  15.5 0.0 all-gather.3.cloned.1.call-start
  15.5 1.1 all-to-all-done
  16.6 0.6 dynamic-slice_bitcast_fusion
  17.2 0.0 all-gather.3.cloned.1.call-update
  17.2 117.6 %all-gather.3.cloned.1.call-done = bf16[128,4,4608]{2,1,0:T(4,128)(2,1)} async-done(((bf16[1,4,4608]{2,1,0:T(4,128)(2,1)}), bf16[128,4,4608]{2,1,0:T(4,128)(2,1)}) %all-gather.3.cloned.1.call-update) | async-done | bytes 4718608 | tf_op jit(solution)/shard_map/all_gather | solution.py:33
  134.8 7.2 %reshape.27 = bf16[512,4608]{1,0:T(8,128)(2,1)} reshape(bf16[128,4,4608]{2,1,0:T(4,128)(2,1)} %all-gather.3.cloned.1.call-done) | data formatting | bytes 9437184
  142.1 6.0 %fusion = f32[256,1024]{1,0:T(8,128)S(1)} fusion(bf16[1024,4608]{1,0:T(8,128)(2,1)} %param.4, bf16[512,4608]{1,0:T(8,128)(2,1)} %reshape.27, s32[]{:T(128)S(6)} %select_n.21), kind=kOutput, calls=%fused_computation | convolution fusion | flops 2415919104 | bytes 12845060 | tf_op jit(solution)/shard_map/dot_general | solution.py:19
  148.0 4.5 %collective-permute-start = (f32[256,1024]{1,0:T(8,128)S(1)}, f32[256,1024]{1,0:T(8,128)S(1)}, u32[]{:S(2)}, u32[]{:S(2)}) collective-permute-start(f32[256,1024]{1,0:T(8,128)S(1)} %fusion), channel_id=1, source_target_pairs={{0,1},{1,0},{2,3},{3,2},{4,5},{5,4},{6,7},{7,6},{8,9},{9,8},{10,11... | collective-permute-start | bytes 3145736 | tf_op jit(solution)/shard_map/ppermute | solution.py:39
  152.5 6.0 %fusion.2 = f32[256,1024]{1,0:T(8,128)S(1)} fusion(bf16[1024,4608]{1,0:T(8,128)(2,1)} %param.4, bf16[512,4608]{1,0:T(8,128)(2,1)} %reshape.27, s32[]{:T(128)S(6)} %select_n.20), kind=kOutput, calls=%fused_computation.2 | convolution fusion | flops 2415919104 | bytes 12845060 | tf_op jit(solution)/shard_map/dot_general | solution.py:19
  158.5 0.0 collective-permute-done
  158.5 1.0 add_convert_fusion
  (2 shorter events, 0.0 us)
Async XLA Ops:
  8.9 7.6 %all-to-all-start = ((bf16[2,2,9216]{2,1,0:T(2,128)(2,1)}), bf16[2,2,9216]{2,1,0:T(2,128)(2,1)S(1)}, u32[]{:S(2)}, u32[]{:S(2)}) async-start(bf16[2,2,9216]{2,1,0:T(2,128)(2,1)} %pad_maximum_fusion), calls=%async_computation | async-start | bytes 147456 | tf_op jit(solution)/shard_map/all_to_all | solution.py:30
  15.5 119.4 %all-gather.3.cloned.1.call-start = ((), (), s32[]{:S(2)}) async-start(), calls=%async_computation.1 | async-start | bytes 4755456 | tf_op jit(solution)/shard_map/all_gather | solution.py:33
  148.0 10.5 %collective-permute-start = (f32[256,1024]{1,0:T(8,128)S(1)}, f32[256,1024]{1,0:T(8,128)S(1)}, u32[]{:S(2)}, u32[]{:S(2)}) collective-permute-start(f32[256,1024]{1,0:T(8,128)S(1)} %fusion), channel_id=1, source_target_pairs={{0,1},{1,0},{2,3},{3,2},{4,5},{5,4},{6,7},{7,6},{8,9},{9,8},{10,11... | collective-permute-start | bytes 3145736 | tf_op jit(solution)/shard_map/ppermute | solution.py:39
Sparse Core Ops, SparseCore 0:
  20.1 114.6 all-gather.2
